TPU v7x, 256 devices: a whole 4x4x8 slice. The times are simulated.
256 devices in a mesh: row: 8 (over z_lo, core), col: 32 (over z_hi, y, x).
Axes of the slice: x: 4, y: 4, z: 8 (z_hi: 2, z_lo: 4; z = z_hi * 4 + z_lo), core: 2. Of those that a mesh axis runs over, the one named last changes fastest.
Arguments:
- tokens: bfloat16 [1024, 12288], P('col', 'row'), may hold values from -6 to 6
- up_weight: bfloat16 [12288, 24576], P('row', 'col'), may hold values from -0.109375 to 0.109375
- down_weight: bfloat16 [24576, 12288], P('col', 'row'), may hold values from -0.078125 to 0.078125
- cotangent: bfloat16 [1024, 12288], P('col', 'row'), may hold values from -6 to 6
- up_pattern: int32 [96, 192], P('row', 'col'), may hold values 0 or 1
- down_pattern: int32 [192, 96], P('col', 'row'), may hold values 0 or 1
Outputs:
- input_grad: bfloat16 [1024, 12288], P('col', 'row')
- up_grad: bfloat16 [12288, 24576], P('row', 'col')
- down_grad: bfloat16 [24576, 12288], P('col', 'row')
All inputs are finite; a program needn't handle non-finite values. No bound on the sum of `up_pattern` or of `down_pattern` on one device may be relied on, other than what follows from the above.
Results may differ from a plain program's by a relative error of at most 0.015.
Values may be sent and summed in bfloat16 or wider, within the bound.
A program may use at most 128 MiB of HBM per device.

v0:
```python
import jax
import jax.numpy as jnp
from jax import lax
from jax.sharding import PartitionSpec as P

half_root = 0.7071067811865476
inv_root_tau = 0.3989422804014327


def widen(pattern, height, breadth):
    blocks_down, blocks_across = pattern.shape
    spread = pattern.astype(jnp.bfloat16)[:, None, :, None]
    spread = jnp.broadcast_to(
        spread, (blocks_down, height // blocks_down, blocks_across, breadth // blocks_across)
    )
    return spread.reshape(height, breadth)


def activate(pre, dact):
    cdf = 0.5 * (1.0 + jax.scipy.special.erf(pre * half_root))
    dens = jnp.exp(-0.5 * pre * pre) * inv_root_tau
    active = (pre * cdf).astype(jnp.bfloat16)
    dhid = (dact * (cdf + pre * dens)).astype(jnp.bfloat16)
    return (active, dhid)


def on_device(tokens, up_weight, down_weight, cotangent, up_pattern, down_pattern):
    full_tokens, full_cotangent = (
        lax.all_gather(tokens, "col", axis=0, tiled=True),
        lax.all_gather(cotangent, "col", axis=0, tiled=True),
    )
    up_mask = widen(up_pattern, up_weight.shape[0], up_weight.shape[1])
    down_mask = widen(down_pattern, down_weight.shape[0], down_weight.shape[1])
    up_eff = up_weight * up_mask
    down_eff = down_weight * down_mask
    pre_part = jnp.dot(full_tokens, up_eff, preferred_element_type=jnp.float32)
    dact_part = lax.dot_general(
        full_cotangent, down_eff, (((1,), (1,)), ((), ())), preferred_element_type=jnp.float32
    )
    pre, dact = lax.psum((pre_part, dact_part), "row")
    active, dhid = activate(pre, dact)
    input_grad = lax.psum_scatter(
        lax.dot_general(
            dhid, up_eff, (((1,), (1,)), ((), ())), preferred_element_type=jnp.float32
        ).astype(jnp.bfloat16),
        "col",
        scatter_dimension=0,
        tiled=True,
    )
    factor = 1.0 / jnp.sqrt(jnp.float32(full_tokens.shape[0]))
    up_grad = lax.dot_general(
        full_tokens, dhid, (((0,), (0,)), ((), ())), preferred_element_type=jnp.float32
    )
    up_grad = (up_grad * up_mask.astype(jnp.float32) * factor).astype(jnp.bfloat16)
    down_grad = lax.dot_general(
        active, full_cotangent, (((0,), (0,)), ((), ())), preferred_element_type=jnp.float32
    )
    down_grad = (down_grad * down_mask.astype(jnp.float32) * factor).astype(jnp.bfloat16)
    return (input_grad, up_grad, down_grad)


def solution(mesh):
    return jax.shard_map(
        on_device,
        mesh=mesh,
        in_specs=(
            P("col", "row"),
            P("row", "col"),
            P("col", "row"),
            P("col", "row"),
            P("row", "col"),
            P("col", "row"),
        ),
        out_specs=(P("col", "row"), P("row", "col"), P("col", "row")),
        check_vma=False,
    )
```

profile of v0, /device:TPU:2, one launch (start us, length us, event | category | flops | bytes accessed | tf_op | source)
XLA Modules:
  0.0 640.0 jit_solution(1797469134917920429)
XLA Ops:
  7.2 0.7 all-gather.5.cloned.1.call-update
  7.9 0.7 all-gather.3.cloned.1.call-update
  8.7 0.7 convert_element_type.28
  9.5 0.9 convert_element_type.27
  10.3 0.5 broadcast_in_dim.5
  10.8 0.4 copy-done.2
  11.2 1.7 fusion.11
  12.9 101.2 %all-gather.5.cloned.1.call-done = bf16[1024,1536]{1,0:T(8,128)(2,1)} async-done(((bf16[32,1536]{1,0:T(8,128)(2,1)}), bf16[1024,1536]{1,0:T(8,128)(2,1)}) %all-gather.5.cloned.1.call-update) | async-done | bytes 3145744 | tf_op jit(solution)/shard_map/all_gather | solution.py:29
  114.1 6.9 %convolution_bitcast_fusion = f32[1024,768]{0,1:T(8,128)} fusion(bf16[1536,768]{1,0:T(8,128)(2,1)} %get-tuple-element.11, bf16[1024,1536]{1,0:T(8,128)(2,1)} %all-gather.5.cloned.1.call-done), kind=kOutput, calls=%fused_computation.18 | convolution fusion | flops 2415919104 | bytes 8650752 | tf_op jit(solution)/shard_map/dot_general | solution.py:36
  121.0 91.3 %all-gather.3.cloned.1.call-done = bf16[1024,1536]{1,0:T(8,128)(2,1)} async-done(((bf16[32,1536]{1,0:T(8,128)(2,1)}), bf16[1024,1536]{1,0:T(8,128)(2,1)}) %all-gather.3.cloned.1.call-update) | async-done | bytes 3145744 | tf_op jit(solution)/shard_map/all_gather | solution.py:30
  212.3 0.5 broadcast_in_dim.4
  212.7 1.7 copy-done
  214.5 0.8 copy-done.5
  215.3 6.0 fusion.9
  221.3 0.2 reduce-scatter.2.cloned.1.call-start
  221.5 143.6 %all-reduce.3.cloned.1.call-done = (f32[1024,768]{0,1:T(8,128)}, f32[1024,768]{0,1:T(8,128)}) async-done(((f32[1024,768]{0,1:T(8,128)}, f32[1024,768]{0,1:T(8,128)}), (f32[1024,768]{0,1:T(8,128)}, f32[1024,768]{0,1:T(8,128)})) %all-reduce.3.cloned.1.call-update) | async-done | bytes 6291472 | tf_op jit(solution)/shard_map/psum | solution.py:40
  365.1 3.6 fusion.7
  368.8 1.1 copy-done.4
  369.9 4.1 convolution_convert_fusion
  374.1 2.4 copy.12
  376.5 7.1 %fusion.1 = bf16[1536,768]{0,1:T(8,128)(2,1)} fusion(bf16[1536,768]{0,1:T(8,128)(2,1)} %copy.12, bf16[1024,768]{0,1:T(8,128)(2,1)} %copy-done.4, bf16[1024,1536]{1,0:T(8,128)(2,1)} %all-gather.5.cloned.1.call-done), kind=kOutput, calls=%fused_computation.3 | convolution fusion | flops 2420637696 | bytes 9437184 | tf_op jit(solution)/shard_map/dot_general | solution.py:51
  383.6 4.4 copy.13
  388.0 6.9 %multiply_convert_fusion = bf16[768,1536]{1,0:T(8,128)(2,1)} fusion(bf16[1024,1536]{1,0:T(8,128)(2,1)} %all-gather.3.cloned.1.call-done, bf16[96,8,12,128]{3,2,1,0:T(8,128)(2,1)S(1)} %bitcast.33, f32[1024,768]{0,1:T(8,128)} %get-tuple-element.10), kind=kOutput, calls=%fused_computation.4 | convolution fusion | flops 2424569856 | bytes 11010048 | tf_op jit(solution)/shard_map/dot_general | solution.py:55
  394.9 238.5 %reduce-scatter.2.cloned.1.call-done = bf16[32,1536]{1,0:T(8,128)(2,1)} async-done(((bf16[1024,1536]{1,0:T(8,128)(2,1)}), bf16[32,1536]{1,0:T(8,128)(2,1)}) %reduce-scatter.2.cloned.1.call-update) | async-done | bytes 98320 | tf_op jit(solution)/shard_map/reduce_scatter | solution.py:42
  (14 shorter events, 0.3 us)
Async XLA Ops:
  7.2 106.9 %all-gather.5.cloned.1.call-start = ((), (), s32[]{:S(2)}) async-start(), calls=%async_computation.2 | async-start | bytes 3244032 | tf_op jit(solution)/shard_map/all_gather | solution.py:29
  7.9 204.4 %all-gather.3.cloned.1.call-start = ((), (), s32[]{:S(2)}) async-start(), calls=%async_computation.1 | async-start | bytes 3244032 | tf_op jit(solution)/shard_map/all_gather | solution.py:30
  8.6 356.5 %all-reduce.3.cloned.1.call-start = ((), (), s32[]{:S(2)}) async-start(), calls=%async_computation.4 | async-start | bytes 12582912 | tf_op jit(solution)/shard_map/psum | solution.py:40
  9.5 1.7 copy-start.2
  212.3 3.0 copy-start.5
  212.7 1.7 copy-start
  221.3 412.1 %reduce-scatter.2.cloned.1.call-start = ((), (), s32[]{:S(2)}) async-start(), calls=%async_computation.3 | async-start | bytes 3244032 | tf_op jit(solution)/shard_map/reduce_scatter | solution.py:42
  365.1 4.8 copy-start.3
  368.8 1.1 copy-start.4
  383.6 4.4 copy-start.1
Sparse Core Ops, SparseCore 0:
  11.5 102.5 all-gather.4
  117.5 94.6 all-gather.2
  221.4 143.6 all-reduce.2
  374.2 259.1 reduce-scatter.1
where the time goes:
time: 640 us
  waiting for transfers between devices  576 us (90%)
  matrix products  31.1 us (5%)
  between operations  13.8 us (2%)
  local copies, waits for them, and re-layouts  11.9 us (2%)
  other arithmetic  6.89 us (1%)
    reduce_scatter x1, waiting for transfers between devices, on_device(): lax.psum_scatter(lax.dot_general(dhid, up_eff, (((1,), (1,)), ((), ())),...  238 us
    psum x1, waiting for transfers between devices, on_device(): pre, dact = lax.psum((pre_part, dact_part), 'row')  144 us
    all_gather x1, waiting for transfers between devices, on_device(): lax.all_gather(tokens, 'col', axis=0, tiled=True)  101 us
    all_gather x1, waiting for transfers between devices, on_device(): lax.all_gather(cotangent, 'col', axis=0, tiled=True)  91.3 us
  transfers between devices with their start and end apart: 4, of which 4 were waited for; matrix products, arithmetic and copies ran while one was open for 5% of the time, Pallas kernels for 0%

commit v1 on v0

--- a/solution.py
+++ b/solution.py
@@ -5,6 +5,11 @@
 
 half_root = 0.7071067811865476
 inv_root_tau = 0.3989422804014327
+
+
+def swapped_in(value, axis, dim):
+    sent = jnp.stack([value] * lax.axis_size(axis))
+    return jnp.concatenate(lax.all_to_all(sent, axis, 0, 0), axis=dim)
 
 
 def widen(pattern, height, breadth):
@@ -26,7 +31,7 @@
 
 def on_device(tokens, up_weight, down_weight, cotangent, up_pattern, down_pattern):
     full_tokens, full_cotangent = (
-        lax.all_gather(tokens, "col", axis=0, tiled=True),
+        swapped_in(tokens, "col", 0),
         lax.all_gather(cotangent, "col", axis=0, tiled=True),
     )
     up_mask = widen(up_pattern, up_weight.shape[0], up_weight.shape[1])

time: 640 us -> 589 us (0.920)
  waiting for transfers between devices: 576 us -> 507 us
  starting transfers between devices: 0.34 us -> 14.7 us
    all_gather x1 -> x0, waiting for transfers between devices: 101 us -> none  [on_device(): lax.all_gather(tokens, 'col', axis=0, tiled=True)]
    all_to_all x0 -> x1, waiting for transfers between devices: none -> 69.5 us  [swapped_in(): return jnp.concatenate(lax.all_to_all(sent, axis, 0, 0), axis=dim)]
    all_gather x1, waiting for transfers between devices: 91.3 us -> 55 us  [on_device(): lax.all_gather(cotangent, 'col', axis=0, tiled=True)]
    all_to_all x0 -> x1, starting transfers between devices: none -> 14.4 us  [swapped_in(): return jnp.concatenate(lax.all_to_all(sent, axis, 0, 0), axis=dim)]
where the time goes in v1:
time: 589 us; the launch traced here: 588 us
  waiting for transfers between devices  507 us (86%)
  matrix products  31.1 us (5%)
  starting transfers between devices  14.7 us (2%)
  local copies, waits for them, and re-layouts  14.5 us (2%)
  between operations  13.8 us (2%)
  other arithmetic  7.02 us (1%)
    reduce_scatter x1, waiting for transfers between devices, on_device(): lax.psum_scatter(lax.dot_general(dhid, up_eff, (((1,), (1,)), ((), ())),...  239 us
    psum x1, waiting for transfers between devices, on_device(): pre, dact = lax.psum((pre_part, dact_part), 'row')  144 us
    all_to_all x1, waiting for transfers between devices, swapped_in(): return jnp.concatenate(lax.all_to_all(sent, axis, 0, 0), axis=dim)  69.5 us
    all_gather x1, waiting for transfers between devices, on_device(): lax.all_gather(cotangent, 'col', axis=0, tiled=True)  55 us
    all_to_all x1, starting transfers between devices, swapped_in(): return jnp.concatenate(lax.all_to_all(sent, axis, 0, 0), axis=dim)  14.4 us
  transfers between devices with their start and end apart: 4, of which 4 were waited for; matrix products, arithmetic and copies ran while one was open for 5% of the time, Pallas kernels for 0%

profile of v1, /device:TPU:2, one launch (start us, length us, event | category | flops | bytes accessed | tf_op | source)
XLA Modules:
  0.0 588.5 jit_solution(4444349977251969583)
XLA Ops:
  7.2 3.0 stack.2
  10.1 14.4 %all-to-all-start = ((bf16[32,32,1536]{2,1,0:T(8,128)(2,1)}), bf16[32,32,1536]{2,1,0:T(8,128)(2,1)}, u32[]{:S(2)}, u32[]{:S(2)}) async-start(bf16[32,32,1536]{2,1,0:T(8,128)(2,1)} %stack.2), calls=%async_computation | async-start | bytes 6291456 | tf_op jit(solution)/shard_map/all_to_all | solution.py:12
  24.6 0.0 all-gather.2.cloned.1.call-start
  24.6 0.7 all-gather.2.cloned.1.call-update
  25.4 0.1 copy.11
  25.5 0.5 broadcast_in_dim.5
  26.0 3.4 fusion.11
  29.3 69.5 %all-to-all-done = bf16[32,32,1536]{2,1,0:T(8,128)(2,1)} async-done(((bf16[32,32,1536]{2,1,0:T(8,128)(2,1)}), bf16[32,32,1536]{2,1,0:T(8,128)(2,1)}, u32[]{:S(2)}, u32[]{:S(2)}) %all-to-all-start) | async-done | bytes 3145760 | tf_op jit(solution)/shard_map/all_to_all | solution.py:12
  98.8 6.9 %convolution_bitcast_fusion = f32[1024,768]{0,1:T(8,128)} fusion(bf16[1536,768]{1,0:T(8,128)(2,1)} %get-tuple-element.11, bf16[1024,1536]{1,0:T(8,128)(2,1)} %bitcast.1), kind=kOutput, calls=%fused_computation.18 | convolution fusion | flops 2415919104 | bytes 8650752 | tf_op jit(solution)/shard_map/dot_general | solution.py:41
  105.7 55.0 %all-gather.2.cloned.1.call-done = bf16[1024,1536]{1,0:T(8,128)(2,1)} async-done(((bf16[32,1536]{1,0:T(8,128)(2,1)}), bf16[1024,1536]{1,0:T(8,128)(2,1)}) %all-gather.2.cloned.1.call-update) | async-done | bytes 3145744 | tf_op jit(solution)/shard_map/all_gather | solution.py:35
  160.7 0.5 broadcast_in_dim.4
  161.2 1.7 copy-done
  162.9 0.8 copy-done.6
  163.7 6.0 %fusion.9 = f32[1024,768]{0,1:T(8,128)} fusion(bf16[1024,1536]{1,0:T(8,128)(2,1)S(1)} %copy-done.6, bf16[768,1536]{1,0:T(8,128)(2,1)} %param.8, bf16[96,8,12,128]{3,2,1,0:T(8,128)(2,1)S(1)} %bitcast.33), kind=kOutput, calls=%fused_computation.17 | convolution fusion | flops 2417098752 | bytes 11010048 | tf_op jit(solution)/shard_map/dot_general | solution.py:42
  169.8 0.2 reduce-scatter.2.cloned.1.call-start
  170.0 143.6 %all-reduce.3.cloned.1.call-done = (f32[1024,768]{0,1:T(8,128)}, f32[1024,768]{0,1:T(8,128)}) async-done(((f32[1024,768]{0,1:T(8,128)}, f32[1024,768]{0,1:T(8,128)}), (f32[1024,768]{0,1:T(8,128)}, f32[1024,768]{0,1:T(8,128)})) %all-reduce.3.cloned.1.call-update) | async-done | bytes 6291472 | tf_op jit(solution)/shard_map/psum | solution.py:45
  313.6 3.6 fusion.7
  317.2 1.1 copy-done.3
  318.4 4.1 convolution_convert_fusion
  322.5 2.4 copy.12
  324.9 7.1 %fusion.1 = bf16[1536,768]{0,1:T(8,128)(2,1)} fusion(bf16[1536,768]{0,1:T(8,128)(2,1)} %copy.12, bf16[1024,768]{0,1:T(8,128)(2,1)} %copy-done.3, bf16[1024,1536]{1,0:T(8,128)(2,1)} %bitcast.1), kind=kOutput, calls=%fused_computation.3 | convolution fusion | flops 2420637696 | bytes 9437184 | tf_op jit(solution)/shard_map/dot_general | solution.py:56
  332.0 4.4 copy.13
  336.5 6.9 %multiply_convert_fusion = bf16[768,1536]{1,0:T(8,128)(2,1)} fusion(bf16[1024,1536]{1,0:T(8,128)(2,1)} %all-gather.2.cloned.1.call-done, bf16[96,8,12,128]{3,2,1,0:T(8,128)(2,1)S(1)} %bitcast.34, f32[1024,768]{0,1:T(8,128)} %get-tuple-element.10), kind=kOutput, calls=%fused_computation.4 | convolution fusion | flops 2424569856 | bytes 11010048 | tf_op jit(solution)/shard_map/dot_general | solution.py:60
  343.4 238.6 %reduce-scatter.2.cloned.1.call-done = bf16[32,1536]{1,0:T(8,128)(2,1)} async-done(((bf16[1024,1536]{1,0:T(8,128)(2,1)}), bf16[32,1536]{1,0:T(8,128)(2,1)}) %reduce-scatter.2.cloned.1.call-update) | async-done | bytes 98320 | tf_op jit(solution)/shard_map/reduce_scatter | solution.py:47
  (16 shorter events, 0.1 us)
Async XLA Ops:
  10.1 15.2 %copy-start.4 = (s32[12,6]{0,1:T(8,128)S(1)}, s32[12,6]{0,1:T(8,128)}, u32[]{:S(2)}) copy-start(s32[12,6]{0,1:T(8,128)} %param.10) | copy-start | bytes 868
  10.1 15.3 %copy-start.5 = (s32[6,12]{1,0:T(8,128)S(1)}, s32[6,12]{1,0:T(8,128)}, u32[]{:S(2)}) copy-start(s32[6,12]{1,0:T(8,128)} %param.11) | copy-start | bytes 868
  10.1 88.7 %all-to-all-start = ((bf16[32,32,1536]{2,1,0:T(8,128)(2,1)}), bf16[32,32,1536]{2,1,0:T(8,128)(2,1)}, u32[]{:S(2)}, u32[]{:S(2)}) async-start(bf16[32,32,1536]{2,1,0:T(8,128)(2,1)} %stack.2), calls=%async_computation | async-start | bytes 6291456 | tf_op jit(solution)/shard_map/all_to_all | solution.py:12
  24.6 136.1 %all-gather.2.cloned.1.call-start = ((), (), s32[]{:S(2)}) async-start(), calls=%async_computation.2 | async-start | bytes 3244032 | tf_op jit(solution)/shard_map/all_gather | solution.py:35
  25.3 288.3 %all-reduce.3.cloned.1.call-start = ((), (), s32[]{:S(2)}) async-start(), calls=%async_computation.4 | async-start | bytes 12582912 | tf_op jit(solution)/shard_map/psum | solution.py:45
  160.7 3.0 copy-start.6
  161.2 1.7 copy-start
  169.8 412.2 %reduce-scatter.2.cloned.1.call-start = ((), (), s32[]{:S(2)}) async-start(), calls=%async_computation.3 | async-start | bytes 3244032 | tf_op jit(solution)/shard_map/reduce_scatter | solution.py:47
  313.6 4.8 copy-start.2
  317.2 1.1 copy-start.3
  332.0 4.4 copy-start.1
Sparse Core Ops, SparseCore 0:
  28.9 131.7 all-gather.1
  169.9 143.6 all-reduce.2
  322.6 259.2 reduce-scatter.1
